TPU v7x, 256 devices: a whole 4x4x8 slice. The times are simulated.
256 devices in a mesh: chan: 32 (over z, x_hi, core), row: 4 (over y), col: 2 (over x_lo).
Axes of the slice: x: 4 (x_hi: 2, x_lo: 2; x = x_hi * 2 + x_lo), y: 4, z: 8, core: 2. Of those that a mesh axis runs over, the one named last changes fastest.
Arguments:
- voltages: bfloat16 [1024, 262144], P('chan', ('row', 'col')), may hold values from -6 to 6
Outputs:
- visibilities: float32 [256, 2, 1024, 1024], P('chan', None, 'row', 'col')
All inputs are finite; a program needn't handle non-finite values.
Results may differ from a plain program's by a relative error of at most 0.0053.
Values may be sent and summed in bfloat16 or wider, within the bound.
No kernel may reach another device: no remote copies, remote signals or barrier semaphores. Data moves between devices by JAX's collectives and lax.ppermute only.
A program may use at most 128 MiB of HBM per device.

v0:
```python
import jax
import jax.numpy as jnp
from jax import lax
from jax.sharding import PartitionSpec as P

FFT_LEN = 512
TAPS = 8
CHANNELS = 256


def shifted(value, axis, by):
    length = lax.axis_size(axis)
    pairs = [(i, i + by) for i in range(length) if 0 <= i + by < length]
    return lax.ppermute(value, axis, pairs)


def window_table(taps, length):
    count = taps * length
    position = jnp.arange(count).astype(jnp.float32)
    offset = (position - count / 2 + 0.5) / length
    taper = 0.5 - 0.5 * jnp.cos(2.0 * jnp.pi * (position + 0.5) / count)
    values = jnp.sinc(offset) * taper
    values = values / jnp.sqrt(jnp.sum(values * values))
    return values.reshape(taps, length)


def fourier_table(channels, length):
    channel_index = jnp.arange(channels, dtype=jnp.int32)[:, None]
    sample_index = jnp.arange(length, dtype=jnp.int32)[None, :]
    phase = (channel_index * sample_index % length).astype(jnp.float32) * (2.0 * jnp.pi / length)
    return jnp.stack([jnp.cos(phase), -jnp.sin(phase)], axis=1).astype(jnp.bfloat16)


def per_device(voltages):
    local_inputs = voltages.shape[0]
    slot_spectra = voltages.shape[1] // FFT_LEN
    window = window_table(TAPS, FFT_LEN)
    table = fourier_table(CHANNELS, FFT_LEN)
    tail = voltages[:, (slot_spectra - TAPS + 1) * FFT_LEN :]
    earlier = shifted(tail, ("row", "col"), 1)
    extended = jnp.concatenate([earlier, voltages], axis=1).reshape(
        local_inputs, slot_spectra + TAPS - 1, FFT_LEN
    )
    total = jnp.zeros((local_inputs, slot_spectra, FFT_LEN), jnp.float32)
    for tap_index in range(TAPS):
        total = total + window[tap_index][None, None, :] * extended[
            :, tap_index : tap_index + slot_spectra, :
        ].astype(jnp.float32)
    filtered = total.astype(jnp.bfloat16)
    spectra = jnp.einsum(
        "kpn,isn->kpsi", table, filtered, preferred_element_type=jnp.float32
    ).astype(jnp.bfloat16)
    turned = lax.all_to_all(spectra, "chan", split_axis=0, concat_axis=3, tiled=True)
    inputs_all = turned.shape[3]
    row_count = lax.axis_size("row")
    col_count = lax.axis_size("col")
    row_block = inputs_all // row_count
    col_block = inputs_all // col_count
    spectra_total = slot_spectra * row_count * col_count
    row_start = lax.axis_index("row") * row_block
    col_start = lax.axis_index("col") * col_block
    piece = lax.all_gather(turned, ("row", "col"), axis=2, tiled=True)
    left = lax.dynamic_slice_in_dim(piece, row_start, row_block, 3)
    right = lax.dynamic_slice_in_dim(piece, col_start, col_block, 3)
    flipped = jnp.stack([left[:, 1], -left[:, 0]], axis=1)
    real_part = jnp.einsum("cpsi,cpsj->cij", left, right, preferred_element_type=jnp.float32)
    imag_part = jnp.einsum("cpsi,cpsj->cij", flipped, right, preferred_element_type=jnp.float32)
    summed = jnp.stack([real_part, imag_part], axis=1)
    return summed / spectra_total


def solution(mesh):
    placed = (P("chan", ("row", "col")),)
    return jax.shard_map(
        per_device,
        mesh=mesh,
        in_specs=placed,
        out_specs=P("chan", None, "row", "col"),
        check_vma=False,
    )
```

profile of v0, /device:TPU:1, one launch (start us, length us, event | category | flops | bytes accessed | tf_op | source)
XLA Modules:
  0.0 496.5 jit_solution(200310706514286712)
XLA Ops:
  6.5 1.0 slice.66
  7.5 4.0 collective-permute-start
  11.5 0.7 multiply_reduce_fusion
  12.2 2.2 negate_convert_fusion
  15.0 0.1 broadcast_divide_fusion
  15.1 0.6 collective-permute-done
  15.7 1.7 pad_maximum_fusion
  17.4 2.6 reshape.97
  20.1 11.7 %convert_bitcast_fusion = bf16[256,2,64,32]{0,2,1,3:T(8,128)(2,1)S(1)} fusion(bf16[32,71,512]{2,1,0:T(8,128)(2,1)} %reshape.97, f32[512]{0:T(512)S(1)} %get-tuple-element.8, f32[512]{0:T(512)S(1)} %get-tuple-element.9, f32[512]{0:T(512)S(1)} %get-tuple-element.10, f32[512]{0:T(512)S(1)} %get-tuple-element.11, f32[512]{0:T(512)S(1)} %get-tuple-element.12, ...), kind=kOutput, calls=%fused_computation.16 | convolution fusion | flops 1101004800 | bytes 19415040 | tf_op jit(solution)/shard_map/kpn,isn->kpsi/dot_general | solution.py:50
  31.8 7.6 %copy.12 = bf16[256,2,64,32]{2,1,3,0:T(2,128)(2,1)} copy(bf16[256,2,64,32]{0,2,1,3:T(8,128)(2,1)S(1)} %convert_bitcast_fusion) | data formatting | bytes 4194304 | tf_op jit(solution)/shard_map/convert_element_type | solution.py:52
  39.5 9.1 %reshape.102 = bf16[32,2,16384]{2,1,0:T(2,128)(2,1)S(1)} reshape(bf16[256,32,2,64]{3,2,1,0:T(2,128)(2,1)} %bitcast.26) | data formatting | bytes 4194304
  48.6 62.7 %all_to_all.18 = bf16[32,2,16384]{2,1,0:T(2,128)(2,1)} all-to-all(bf16[32,2,16384]{2,1,0:T(2,128)(2,1)S(1)} %reshape.102), channel_id=1, replica_groups=mesh['chan'=32,'row'=4,'col'=2] {'chan'}, dimensions={0} | all-to-all | bytes 4194304 | tf_op jit(solution)/shard_map/all_to_all | solution.py:53
  111.3 9.8 %reshape.103 = bf16[256,32,2,64]{3,2,1,0:T(2,128)(2,1)} reshape(bf16[32,2,16384]{2,1,0:T(2,128)(2,1)} %all_to_all.18) | data formatting | bytes 4194304
  121.1 3.2 copy.13
  124.3 2.9 copy.14
  127.2 4.8 copy.15
  132.0 0.0 all-gather.2.cloned.1.call-update
  132.0 327.7 %all-gather.2.cloned.1.call-done = bf16[8,2,512,1024]{3,2,1,0:T(8,128)(2,1)} async-done(((bf16[8,2,64,1024]{3,2,1,0:T(8,128)(2,1)}), bf16[8,2,512,1024]{3,2,1,0:T(8,128)(2,1)}) %all-gather.2.cloned.1.call-update) | async-done | bytes 16777232 | tf_op jit(solution)/shard_map/all_gather | solution.py:62
  459.7 4.1 constant_dynamic-slice_fusion
  463.8 9.4 %fusion.8 = f32[8,1,256,512]{3,2,0,1:T(8,128)} fusion(bf16[8,2,512,1024]{3,2,1,0:T(8,128)(2,1)} %all-gather.2.cloned.1.call-done, s32[]{:T(128)S(6)} %select_n.65, s32[]{:T(128)S(6)} %select_n.64), kind=kOutput, calls=%fused_computation.11 | convolution fusion | flops 2147483648 | bytes 16777224 | tf_op jit(solution)/shard_map/cpsi,cpsj->cij/dot_general | solution.py:66
  473.2 1.6 copy-done
  474.7 6.0 %fusion.13 = f32[8,1,256,512]{3,2,0,1:T(8,128)} fusion(bf16[8,2,512,1024]{3,2,1,0:T(8,128)(2,1)S(1)} %copy-done, s32[]{:T(128)S(6)} %select_n.65, bf16[8,1,512,256]{3,2,1,0:T(8,128)(2,1)} %get-tuple-element.6, bf16[8,1,512,256]{3,2,1,0:T(8,128)(2,1)S(1)} %get-tuple-element.5), kind=kOutput, calls=%fused_computation.12 | convolution fusion | flops 2149580800 | bytes 16777220 | tf_op jit(solution)/shard_map/cpsi,cpsj->cij/dot_general | solution.py:67
  480.7 4.5 maximum_multiply_fusion
  485.2 4.4 copy.18
  (3 shorter events, 0.0 us)
Async XLA Ops:
  6.5 453.2 %all-gather.2.cloned.1.call-start = ((), (), s32[]{:S(2)}) async-start(), calls=%async_computation.1 | async-start | bytes 18874368 | tf_op jit(solution)/shard_map/all_gather | solution.py:62
  7.5 8.2 %collective-permute-start = (bf16[32,3584]{1,0:T(8,128)(2,1)S(1)}, bf16[32,3584]{1,0:T(8,128)(2,1)S(1)}, u32[]{:S(2)}, u32[]{:S(2)}) collective-permute-start(bf16[32,3584]{1,0:T(8,128)(2,1)S(1)} %slice.66), channel_id=1, source_target_pairs={{0,1},{1,2},{2,3},{3,4},{4,5},{5,6},{6,7},{8,9},{9,10},{10,11},{11... | collective-permute-start | bytes 688136 | tf_op jit(solution)/shard_map/ppermute | solution.py:14
  463.8 10.9 %copy-start = (bf16[8,2,512,1024]{3,2,1,0:T(8,128)(2,1)S(1)}, bf16[8,2,512,1024]{3,2,1,0:T(8,128)(2,1)}, u32[]{:S(2)}) copy-start(bf16[8,2,512,1024]{3,2,1,0:T(8,128)(2,1)} %all-gather.2.cloned.1.call-done) | copy-start | bytes 50331652
Sparse Core Ops, SparseCore 0:
  132.1 327.5 all-gather.1
where the time goes:
time: 497 us
  waiting for transfers between devices  328 us (66%)
  blocking collectives  62.7 us (13%)
  local copies, waits for them, and re-layouts  47.1 us (9%)
  matrix products  27.1 us (5%)
  between operations  14.2 us (3%)
  other arithmetic  13.3 us (3%)
    all_gather x1, waiting for transfers between devices, per_device(): piece = lax.all_gather(turned, ('row', 'col'), axis=2, tiled=True)  328 us
    all_to_all x1, blocking collectives, per_device(): lax.all_to_all(spectra, 'chan', split_axis=0, concat_axis=3, tiled=True)  62.7 us
    unnamed x4, local copies, waits for them, and re-layouts  20.5 us
    dot_general x1, matrix products, per_device(): jnp.einsum('kpn,isn->kpsi', table, filtered, preferred_element_type=jnp.f...  11.7 us
    all_to_all x3, local copies, waits for them, and re-layouts, per_device(): lax.all_to_all(spectra, 'chan', split_axis=0, concat_axis=3, tiled=True)  10.9 us
  transfers between devices with their start and end apart: 2, of which 2 were waited for; matrix products, arithmetic and copies ran while one was open for 1% of the time, Pallas kernels for 0%

commit v1 on v0

--- a/solution.py
+++ b/solution.py
@@ -50,7 +50,10 @@
     spectra = jnp.einsum(
         "kpn,isn->kpsi", table, filtered, preferred_element_type=jnp.float32
     ).astype(jnp.bfloat16)
-    turned = lax.all_to_all(spectra, "chan", split_axis=0, concat_axis=3, tiled=True)
+    turned = jnp.concatenate(
+        lax.all_to_all(jnp.stack(jnp.split(spectra, lax.axis_size("chan"), axis=0)), "chan", 0, 0),
+        axis=3,
+    )
     inputs_all = turned.shape[3]
     row_count = lax.axis_size("row")
     col_count = lax.axis_size("col")

time: 497 us -> 601 us (1.21)
  local copies, waits for them, and re-layouts: 47.1 us -> 149 us
    another operation x0 -> x35, local copies, waits for them, and re-layouts: none -> 82.4 us  [per_device(): jnp.stack(jnp.split(spectra, lax.axis_size('chan'), axis=0))]
    unnamed x4 -> x67, local copies, waits for them, and re-layouts: 20.5 us -> 47.8 us
    all_to_all x3 -> x0, local copies, waits for them, and re-layouts: 10.9 us -> none  [per_device(): lax.all_to_all(spectra, 'chan', split_axis=0, concat_axis=3, tiled=True)]
    reshape x0 -> x3, local copies, waits for them, and re-layouts: none -> 10.9 us  [per_device(): jnp.concatenate(lax.all_to_all(jnp.stack(jnp.split(spectra, lax.axis_size...]
    convert_element_type x1 -> x0, local copies, waits for them, and re-layouts: 7.64 us -> none  [per_device(): spectra = jnp.einsum('kpn,isn->kpsi', table, filtered, preferred_element_...]
  transfers between devices with their start and end apart: 2 -> 2, of which waited for: 2 -> 2; matrix products, arithmetic and copies ran while one was open for 1% -> 0% of each run, Pallas kernels for 0% -> 0%
where the time goes in v1:
time: 601 us; the launch traced here: 599 us
  waiting for transfers between devices  328 us (55%)
  local copies, waits for them, and re-layouts  149 us (25%)
  blocking collectives  62.8 us (10%)
  matrix products  27 us (4%)
  between operations  14.3 us (2%)
  other arithmetic  13.3 us (2%)
    all_gather x1, waiting for transfers between devices, per_device(): piece = lax.all_gather(turned, ('row', 'col'), axis=2, tiled=True)  328 us
    another operation x35, local copies, waits for them, and re-layouts, per_device(): jnp.stack(jnp.split(spectra, lax.axis_size('chan'), axis=0))  82.4 us
    all_to_all x1, blocking collectives, per_device(): lax.all_to_all(jnp.stack(jnp.split(spectra, lax.axis_size('chan'), axis=0...  62.8 us
    unnamed x67, local copies, waits for them, and re-layouts  47.8 us
  transfers between devices with their start and end apart: 2, of which 2 were waited for; matrix products, arithmetic and copies ran while one was open for 0% of the time, Pallas kernels for 0%

profile of v1, /device:TPU:1, one launch (start us, length us, event | category | flops | bytes accessed | tf_op | source)
XLA Modules:
  0.0 598.6 jit_solution(12417597769974413305)
XLA Ops:
  7.5 4.0 collective-permute-start
  17.4 2.6 reshape.103
  20.1 11.6 %convert_bitcast_fusion = bf16[256,2,64,32]{0,2,1,3:T(8,128)(2,1)S(1)} fusion(bf16[32,71,512]{2,1,0:T(8,128)(2,1)} %reshape.103, f32[512]{0:T(512)S(1)} %get-tuple-element.40, f32[512]{0:T(512)S(1)} %get-tuple-element.41, f32[512]{0:T(512)S(1)} %get-tuple-element.42, f32[512]{0:T(512)S(1)} %get-tuple-element.43, f32[512]{0:T(512)S(1)} %get-tuple-element.44, ...), kind=kOutput, calls=%fused_computation.16 | convolution fusion | flops 1101004800 | bytes 19415040 | tf_op jit(solution)/shard_map/kpn,isn->kpsi/dot_general | solution.py:50
  31.7 6.7 %slice_bitcast_fusion.19 = (bf16[1,8,2,64,32]{1,3,2,4,0:T(8,128)(2,1)}, bf16[1,8,2,64,32]{1,3,2,4,0:T(8,128)(2,1)}, bf16[1,8,2,64,32]{1,3,2,4,0:T(8,128)(2,1)}, ...) fusion(bf16[256,2,64,32]{0,2,1,3:T(8,128)(2,1)S(1)} %convert_bi, ...), kind=kLoop, calls=%fused_computation.36 | loop fusion | bytes 1703936 | tf_op jit(solution)/shard_map/stack | solution.py:54
  38.4 8.9 %slice_bitcast_fusion = (bf16[1,8,2,64,32]{1,3,2,4,0:T(8,128)(2,1)}, bf16[1,8,2,64,32]{1,3,2,4,0:T(8,128)(2,1)}, bf16[1,8,2,64,32]{1,3,2,4,0:T(8,128)(2,1)}, bf1...) fusion(bf16[256,2,64,32]{0,2,1,3:T(8,128)(2,1)S(1)} %convert_bi, ...), kind=kLoop, calls=%fused_computation.17 | loop fusion | bytes 2490368 | tf_op jit(solution)/shard_map/stack | solution.py:54
  47.3 2.3 copy.58
  49.6 2.3 copy.57
  58.6 2.3 copy.53
  67.7 2.3 copy.49
  69.9 2.3 copy.48
  83.8 2.3 copy.73
  97.4 2.3 copy.67
  145.7 6.9 %reshape.110 = bf16[32,2,16384]{2,1,0:T(2,128)(2,1)S(1)} reshape(bf16[32,8,2,32,64]{4,3,2,1,0:T(8,128)(2,1)} %bitcast.91) | data formatting | bytes 4194304
  152.6 62.8 %all_to_all.5 = bf16[32,2,16384]{2,1,0:T(2,128)(2,1)} all-to-all(bf16[32,2,16384]{2,1,0:T(2,128)(2,1)S(1)} %reshape.110), channel_id=1, replica_groups=mesh['chan'=32,'row'=4,'col'=2] {'chan'}, dimensions={0} | all-to-all | bytes 4194304 | tf_op jit(solution)/shard_map/all_to_all | solution.py:54
  215.4 7.9 %reshape.111 = bf16[32,8,2,32,64]{4,3,2,1,0:T(8,128)(2,1)} reshape(bf16[32,2,16384]{2,1,0:T(2,128)(2,1)} %all_to_all.5) | data formatting | bytes 4194304
  223.4 3.2 bitcast_bitcast_fusion
  226.5 2.9 copy.78
  229.4 4.8 copy.79
  234.2 327.5 %all-gather.2.cloned.1.call-done = bf16[8,2,512,1024]{3,2,1,0:T(8,128)(2,1)} async-done(((bf16[8,2,64,1024]{3,2,1,0:T(8,128)(2,1)}), bf16[8,2,512,1024]{3,2,1,0:T(8,128)(2,1)}) %all-gather.2.cloned.1.call-update) | async-done | bytes 16777232 | tf_op jit(solution)/shard_map/all_gather | solution.py:65
  561.8 4.1 constant_dynamic-slice_fusion
  565.9 9.4 %fusion.8 = f32[8,1,256,512]{3,2,0,1:T(8,128)} fusion(bf16[8,2,512,1024]{3,2,1,0:T(8,128)(2,1)} %all-gather.2.cloned.1.call-done, s32[]{:T(128)S(6)} %select_n.65, s32[]{:T(128)S(6)} %select_n.64), kind=kOutput, calls=%fused_computation.11 | convolution fusion | flops 2147483648 | bytes 16777224 | tf_op jit(solution)/shard_map/cpsi,cpsj->cij/dot_general | solution.py:69
  576.8 6.0 %fusion.13 = f32[8,1,256,512]{3,2,0,1:T(8,128)} fusion(bf16[8,2,512,1024]{3,2,1,0:T(8,128)(2,1)S(1)} %copy-done, s32[]{:T(128)S(6)} %select_n.65, bf16[8,1,512,256]{3,2,1,0:T(8,128)(2,1)} %get-tuple-element.6, bf16[8,1,512,256]{3,2,1,0:T(8,128)(2,1)S(1)} %get-tuple-element.5), kind=kOutput, calls=%fused_computation.12 | convolution fusion | flops 2149580800 | bytes 16777220 | tf_op jit(solution)/shard_map/cpsi,cpsj->cij/dot_general | solution.py:70
  582.8 4.5 maximum_multiply_fusion
  587.3 4.4 copy.82
  (100 shorter events, 90.2 us)
Async XLA Ops:
  6.5 555.2 %all-gather.2.cloned.1.call-start = ((), (), s32[]{:S(2)}) async-start(), calls=%async_computation.1 | async-start | bytes 18874368 | tf_op jit(solution)/shard_map/all_gather | solution.py:65
  7.5 8.2 %collective-permute-start = (bf16[32,3584]{1,0:T(8,128)(2,1)S(1)}, bf16[32,3584]{1,0:T(8,128)(2,1)S(1)}, u32[]{:S(2)}, u32[]{:S(2)}) collective-permute-start(bf16[32,3584]{1,0:T(8,128)(2,1)S(1)} %slice.66), channel_id=1, source_target_pairs={{0,1},{1,2},{2,3},{3,4},{4,5},{5,6},{6,7},{8,9},{9,10},{10,11},{11... | collective-permute-start | bytes 688136 | tf_op jit(solution)/shard_map/ppermute | solution.py:14
  112.0 14.8 %copy-start.10 = (bf16[1,8,2,64,32]{3,4,2,1,0:T(8,128)(2,1)S(1)}, bf16[1,8,2,64,32]{3,4,2,1,0:T(8,128)(2,1)}, u32[]{:S(2)}) copy-start(bf16[1,8,2,64,32]{3,4,2,1,0:T(8,128)(2,1)} %copy.55) | copy-start | bytes 196612
  112.0 15.4 %copy-start.8 = (bf16[1,8,2,64,32]{3,4,2,1,0:T(8,128)(2,1)S(1)}, bf16[1,8,2,64,32]{3,4,2,1,0:T(8,128)(2,1)}, u32[]{:S(2)}) copy-start(bf16[1,8,2,64,32]{3,4,2,1,0:T(8,128)(2,1)} %copy.56) | copy-start | bytes 196612
  112.0 16.1 %copy-start.6 = (bf16[1,8,2,64,32]{3,4,2,1,0:T(8,128)(2,1)S(1)}, bf16[1,8,2,64,32]{3,4,2,1,0:T(8,128)(2,1)}, u32[]{:S(2)}) copy-start(bf16[1,8,2,64,32]{3,4,2,1,0:T(8,128)(2,1)} %copy.57) | copy-start | bytes 196612
  112.0 16.7 %copy-start.4 = (bf16[1,8,2,64,32]{3,4,2,1,0:T(8,128)(2,1)S(1)}, bf16[1,8,2,64,32]{3,4,2,1,0:T(8,128)(2,1)}, u32[]{:S(2)}) copy-start(bf16[1,8,2,64,32]{3,4,2,1,0:T(8,128)(2,1)} %copy.58) | copy-start | bytes 196612
  112.0 27.7 %copy-start.9 = (bf16[1,8,2,64,32]{3,4,2,1,0:T(8,128)(2,1)S(1)}, bf16[1,8,2,64,32]{3,4,2,1,0:T(8,128)(2,1)}, u32[]{:S(2)}) copy-start(bf16[1,8,2,64,32]{3,4,2,1,0:T(8,128)(2,1)} %copy.69) | copy-start | bytes 196612
  112.0 28.3 %copy-start.7 = (bf16[1,8,2,64,32]{3,4,2,1,0:T(8,128)(2,1)S(1)}, bf16[1,8,2,64,32]{3,4,2,1,0:T(8,128)(2,1)}, u32[]{:S(2)}) copy-start(bf16[1,8,2,64,32]{3,4,2,1,0:T(8,128)(2,1)} %copy.70) | copy-start | bytes 196612
  112.1 29.0 %copy-start.5 = (bf16[1,8,2,64,32]{3,4,2,1,0:T(8,128)(2,1)S(1)}, bf16[1,8,2,64,32]{3,4,2,1,0:T(8,128)(2,1)}, u32[]{:S(2)}) copy-start(bf16[1,8,2,64,32]{3,4,2,1,0:T(8,128)(2,1)} %copy.71) | copy-start | bytes 196612
  112.1 29.7 %copy-start.3 = (bf16[1,8,2,64,32]{3,4,2,1,0:T(8,128)(2,1)S(1)}, bf16[1,8,2,64,32]{3,4,2,1,0:T(8,128)(2,1)}, u32[]{:S(2)}) copy-start(bf16[1,8,2,64,32]{3,4,2,1,0:T(8,128)(2,1)} %copy.72) | copy-start | bytes 196612
  113.1 22.6 %copy-start.16 = (bf16[1,8,2,64,32]{3,4,2,1,0:T(8,128)(2,1)S(1)}, bf16[1,8,2,64,32]{3,4,2,1,0:T(8,128)(2,1)}, u32[]{:S(2)}) copy-start(bf16[1,8,2,64,32]{3,4,2,1,0:T(8,128)(2,1)} %copy.63) | copy-start | bytes 196612
  113.1 23.2 %copy-start.15 = (bf16[1,8,2,64,32]{3,4,2,1,0:T(8,128)(2,1)S(1)}, bf16[1,8,2,64,32]{3,4,2,1,0:T(8,128)(2,1)}, u32[]{:S(2)}) copy-start(bf16[1,8,2,64,32]{3,4,2,1,0:T(8,128)(2,1)} %copy.64) | copy-start | bytes 196612
  113.1 23.9 %copy-start.14 = (bf16[1,8,2,64,32]{3,4,2,1,0:T(8,128)(2,1)S(1)}, bf16[1,8,2,64,32]{3,4,2,1,0:T(8,128)(2,1)}, u32[]{:S(2)}) copy-start(bf16[1,8,2,64,32]{3,4,2,1,0:T(8,128)(2,1)} %copy.65) | copy-start | bytes 196612
  113.1 24.6 %copy-start.13 = (bf16[1,8,2,64,32]{3,4,2,1,0:T(8,128)(2,1)S(1)}, bf16[1,8,2,64,32]{3,4,2,1,0:T(8,128)(2,1)}, u32[]{:S(2)}) copy-start(bf16[1,8,2,64,32]{3,4,2,1,0:T(8,128)(2,1)} %copy.66) | copy-start | bytes 196612
  113.1 25.2 %copy-start.12 = (bf16[1,8,2,64,32]{3,4,2,1,0:T(8,128)(2,1)S(1)}, bf16[1,8,2,64,32]{3,4,2,1,0:T(8,128)(2,1)}, u32[]{:S(2)}) copy-start(bf16[1,8,2,64,32]{3,4,2,1,0:T(8,128)(2,1)} %copy.67) | copy-start | bytes 196612
  113.2 25.9 %copy-start.11 = (bf16[1,8,2,64,32]{3,4,2,1,0:T(8,128)(2,1)S(1)}, bf16[1,8,2,64,32]{3,4,2,1,0:T(8,128)(2,1)}, u32[]{:S(2)}) copy-start(bf16[1,8,2,64,32]{3,4,2,1,0:T(8,128)(2,1)} %copy.68) | copy-start | bytes 196612
  113.2 29.2 %copy-start.2 = (bf16[1,8,2,64,32]{3,4,2,1,0:T(8,128)(2,1)S(1)}, bf16[1,8,2,64,32]{3,4,2,1,0:T(8,128)(2,1)}, u32[]{:S(2)}) copy-start(bf16[1,8,2,64,32]{3,4,2,1,0:T(8,128)(2,1)} %copy.73) | copy-start | bytes 196612
  113.2 29.9 %copy-start.1 = (bf16[1,8,2,64,32]{3,4,2,1,0:T(8,128)(2,1)S(1)}, bf16[1,8,2,64,32]{3,4,2,1,0:T(8,128)(2,1)}, u32[]{:S(2)}) copy-start(bf16[1,8,2,64,32]{3,4,2,1,0:T(8,128)(2,1)} %copy.74) | copy-start | bytes 196612
  565.9 10.9 %copy-start = (bf16[8,2,512,1024]{3,2,1,0:T(8,128)(2,1)S(1)}, bf16[8,2,512,1024]{3,2,1,0:T(8,128)(2,1)}, u32[]{:S(2)}) copy-start(bf16[8,2,512,1024]{3,2,1,0:T(8,128)(2,1)} %all-gather.2.cloned.1.call-done) | copy-start | bytes 50331652
Sparse Core Ops, SparseCore 0:
  234.4 327.3 all-gather.1
